TPU v7x, 128 devices: a whole 4x4x4 slice. The times are simulated.
128 devices in a mesh: leaf: 4 (over y), rows: 32 (over z, x, core).
Axes of the slice: x: 4, y: 4, z: 4, core: 2. Of those that a mesh axis runs over, the one named last changes fastest.
Arguments:
- leaf_rhs: float32 [8, 16, 2048], P(None, 'leaf', 'rows'), may hold values from -6 to 6
- parent_rhs: float32 [8, 4, 4096], P(None, 'leaf', 'rows'), may hold values from -6 to 6
- root_rhs: float32 [8, 4096], P(None, ('leaf', 'rows')), may hold values from -6 to 6
- leaf_inv: bfloat16 [16, 2048, 2048], P('leaf', 'rows'), as said below
- leaf_panel: bfloat16 [16, 8192, 2048], P('leaf', 'rows'), may hold values from -0.0625 to 0.0625
- leaf_rows: int32 [16, 8192], P('leaf', 'rows'), may hold values from 0 to 8191, as said below
- leaf_height: int32 [16], P('leaf'), may hold values from 2048 to 8192
- parent_inv: bfloat16 [4, 4096, 4096], P('leaf', 'rows'), as said below
- parent_panel: bfloat16 [4, 4096, 4096], P('leaf', 'rows'), may hold values from -0.046875 to 0.046875
- parent_rows: int32 [4, 4096], P('leaf', 'rows'), may hold values from 0 to 4095, as said below
- parent_height: int32 [4], P('leaf'), may hold values from 1024 to 4096
- root_inv: bfloat16 [4096, 4096], P('rows'), as said below
Outputs:
- leaf_solution: float32 [8, 16, 2048], P(None, 'leaf', 'rows')
- parent_solution: float32 [8, 4, 4096], P(None, 'leaf', 'rows')
- root_solution: float32 [8, 4096], P(None, ('leaf', 'rows'))
Inputs may be any that keep to these rules, and one draw needn't show every extreme that they name: `leaf_rows`: each leaf's first leaf_height entries are distinct and ascending; every entry is a valid ancestor index. `parent_rows`: each parent's first parent_height entries are distinct and ascending. `leaf_inv`: A dense well conditioned matrix. `parent_inv`: A dense well conditioned matrix. `root_inv`: A dense well conditioned matrix.
All inputs are finite; a program needn't handle non-finite values.
Results may differ from a plain program's by a relative error of at most 0.009.
Values may be sent and summed in bfloat16 or wider, within the bound.
A program may use at most 64 MiB of HBM per device.

v0:
```python
import jax
import jax.numpy as jnp
from jax import lax
from jax.sharding import PartitionSpec as P


def shards(
    leaf_rhs,
    parent_rhs,
    root_rhs,
    leaf_inv,
    leaf_panel,
    leaf_rows,
    leaf_height,
    parent_inv,
    parent_panel,
    parent_rows,
    parent_height,
    root_inv,
):
    rcount = leaf_rhs.shape[0]
    group_leaves = leaf_rhs.shape[1]
    leaf_local = leaf_panel.shape[1]
    parent_width = parent_inv.shape[2]
    root_width = root_inv.shape[1]
    row_index = lax.axis_index("rows")
    parent_cols = parent_rhs.shape[2]
    root_cols = root_rhs.shape[1]
    flat_index = lax.axis_index("leaf") * lax.axis_size("rows") + row_index
    block = leaf_inv
    ly = jnp.einsum(
        "rln,lin->rli",
        lax.all_gather(leaf_rhs.astype(jnp.bfloat16), "rows", axis=2, tiled=True),
        block,
        preferred_element_type=jnp.float32,
    )
    lyb = ly.astype(jnp.bfloat16)
    block = leaf_panel
    lupd = jnp.einsum(
        "rln,lhn->rlh",
        lax.all_gather(lyb, "rows", axis=2, tiled=True),
        block,
        preferred_element_type=jnp.float32,
    )
    leaf_pos = row_index * leaf_local + jnp.arange(leaf_local, dtype=jnp.int32)
    leaf_mask = leaf_pos[None, :] < leaf_height[:, None]
    lupd = jnp.where(leaf_mask[None, :, :], lupd, 0.0)
    leaf_flat = leaf_rows.reshape(-1)
    local_acc = (
        jnp.zeros((rcount, parent_width + root_width), jnp.float32)
        .at[:, leaf_flat]
        .add(lupd.reshape(rcount, -1))
    )
    group_acc = lax.psum(local_acc, "rows")
    parent_acc = group_acc[:, :parent_width]
    root_from_leaves = lax.psum(group_acc[:, parent_width:], "leaf")
    parent_slice = lax.dynamic_slice_in_dim(parent_acc, row_index * parent_cols, parent_cols, 1)
    prb = (parent_rhs[:, 0, :] - parent_slice).astype(jnp.bfloat16)
    inverse_rows = parent_inv[0]
    panel_rows = parent_panel[0]
    block = inverse_rows
    py = jnp.dot(
        lax.all_gather(prb, "rows", axis=1, tiled=True), block.T, preferred_element_type=jnp.float32
    )
    pyb = py.astype(jnp.bfloat16)
    parent_local = panel_rows.shape[0]
    block = panel_rows
    pupd = jnp.dot(
        lax.all_gather(pyb, "rows", axis=1, tiled=True), block.T, preferred_element_type=jnp.float32
    )
    parent_pos = row_index * parent_local + jnp.arange(parent_local, dtype=jnp.int32)
    parent_mask = parent_pos < parent_height[0]
    pupd = jnp.where(parent_mask[None, :], pupd, 0.0)
    parent_root = jnp.zeros((rcount, root_width), jnp.float32).at[:, parent_rows[0]].add(pupd)
    root_acc = root_from_leaves + lax.psum(parent_root, ("leaf", "rows"))
    root_slice = lax.dynamic_slice_in_dim(root_acc, flat_index * root_cols, root_cols, 1)
    rrb = (root_rhs - root_slice).astype(jnp.bfloat16)
    block = root_inv
    ry = jnp.dot(
        lax.all_gather(rrb, ("leaf", "rows"), axis=1, tiled=True),
        block.T,
        preferred_element_type=jnp.float32,
    )
    root_term = jnp.dot(ry.astype(jnp.bfloat16), root_inv, preferred_element_type=jnp.float32)
    root_full = lax.psum(root_term, "rows")
    root_solution = lax.dynamic_slice_in_dim(root_full, flat_index * root_cols, root_cols, 1)
    rxb = root_full.astype(jnp.bfloat16)
    parent_anc = rxb[:, parent_rows[0]]
    parent_anc = jnp.where(parent_mask[None, :], parent_anc, jnp.zeros_like(parent_anc))
    parent_term = jnp.dot(parent_anc, panel_rows, preferred_element_type=jnp.float32)
    parent_tail = lax.psum_scatter(parent_term, "rows", scatter_dimension=1, tiled=True)
    pvb = (py - parent_tail).astype(jnp.bfloat16)
    parent_sol_term = jnp.dot(pvb, inverse_rows, preferred_element_type=jnp.float32)
    parent_sol = lax.psum_scatter(parent_sol_term, "rows", scatter_dimension=1, tiled=True)
    parent_whole = lax.all_gather(parent_sol.astype(jnp.bfloat16), "rows", axis=1, tiled=True)
    ancestors = jnp.concatenate([parent_whole, rxb], axis=1)
    leaf_anc = ancestors[:, leaf_flat].reshape(rcount, group_leaves, leaf_local)
    leaf_anc = jnp.where(leaf_mask[None, :, :], leaf_anc, jnp.zeros_like(leaf_anc))
    leaf_term = jnp.einsum("rlh,lhc->rlc", leaf_anc, leaf_panel, preferred_element_type=jnp.float32)
    leaf_tail = lax.psum_scatter(leaf_term, "rows", scatter_dimension=2, tiled=True)
    lvb = (ly - leaf_tail).astype(jnp.bfloat16)
    leaf_sol_term = jnp.einsum("rli,lic->rlc", lvb, leaf_inv, preferred_element_type=jnp.float32)
    leaf_sol = lax.psum_scatter(leaf_sol_term, "rows", scatter_dimension=2, tiled=True)
    return (leaf_sol, parent_sol[:, None, :], root_solution)


def solution(mesh):
    return jax.shard_map(
        shards,
        mesh=mesh,
        in_specs=(
            P(None, "leaf", "rows"),
            P(None, "leaf", "rows"),
            P(None, ("leaf", "rows")),
            P("leaf", "rows", None),
            P("leaf", "rows", None),
            P("leaf", "rows"),
            P("leaf"),
            P("leaf", "rows", None),
            P("leaf", "rows", None),
            P("leaf", "rows"),
            P("leaf"),
            P("rows", None),
        ),
        out_specs=(P(None, "leaf", "rows"), P(None, "leaf", "rows"), P(None, ("leaf", "rows"))),
        check_vma=False,
    )
```

profile of v0, /device:TPU:0, one launch (start us, length us, event | category | flops | bytes accessed | tf_op | source)
XLA Modules:
  0.0 916.0 jit_solution(10626270217796478974)
XLA Ops:
  8.9 27.5 %all_gather.18 = bf16[8,4,2048]{0,1,2:T(4,128)(2,1)S(1)} all-gather(bf16[8,4,64]{0,1,2:T(4,128)(2,1)S(1)} %copy.62), channel_id=1, replica_groups=mesh['leaf'=4,'rows'=32] {'rows'}, dimensions={2}, use_global_device_ids=true | all-gather | bytes 135168 | tf_op jit(solution)/shard_map/all_gather | solution.py:33
  37.3 25.3 %all_gather.19 = bf16[8,4,2048]{0,1,2:T(4,128)(2,1)S(1)} all-gather(bf16[8,4,64]{0,1,2:T(4,128)(2,1)S(1)} %copy.64), channel_id=1, replica_groups=mesh['leaf'=4,'rows'=32] {'rows'}, dimensions={2}, use_global_device_ids=true | all-gather | bytes 135168 | tf_op jit(solution)/shard_map/all_gather | solution.py:41
  62.7 3.4 fusion.6
  66.3 8.2 scatter_custom_fusion
  74.5 3.5 copy.67
  78.9 100.7 %all-reduce.5.cloned.1.call-done = f32[8,8192]{1,0:T(8,128)} async-done(((f32[8,8192]{1,0:T(8,128)}), f32[8,8192]{1,0:T(8,128)}) %all-reduce.5.cloned.1.call-update) | async-done | bytes 262160 | tf_op jit(solution)/shard_map/psum | solution.py:54
  179.6 1.6 fusion.35
  181.2 24.6 %all_gather.20 = bf16[8,4096]{1,0:T(8,128)(2,1)S(1)} all-gather(bf16[8,128]{1,0:T(8,128)(2,1)S(1)} %subtract_convert_fusion.3), channel_id=1, replica_groups=mesh['leaf'=4,'rows'=32] {'rows'}, dimensions={1}, use_global_device_ids=true | all-gather | bytes 67584 | tf_op jit(solution)/shard_map/all_gather | solution.py:63
  206.2 21.5 %all_gather.21 = bf16[8,4096]{1,0:T(8,128)(2,1)S(1)} all-gather(bf16[8,128]{1,0:T(8,128)(2,1)S(1)} %get-tuple-element.22), channel_id=1, replica_groups=mesh['leaf'=4,'rows'=32] {'rows'}, dimensions={1}, use_global_device_ids=true | all-gather | bytes 67584 | tf_op jit(solution)/shard_map/all_gather | solution.py:69
  228.3 1.5 scatter_custom_fusion.1
  229.8 1.2 copy.69
  231.8 141.0 %all-reduce.9.cloned.1.call-done = f32[8,4096]{1,0:T(8,128)} async-done(((f32[8,4096]{1,0:T(8,128)}), f32[8,4096]{1,0:T(8,128)}) %all-reduce.9.cloned.1.call-update) | async-done | bytes 131088 | tf_op jit(solution)/shard_map/psum | solution.py:75
  372.8 41.1 %all-reduce.7.cloned.1.call-done = f32[8,4096]{1,0:T(8,128)} async-done(((f32[8,4096]{1,0:T(8,128)}), f32[8,4096]{1,0:T(8,128)}) %all-reduce.7.cloned.1.call-update) | async-done | bytes 131088 | tf_op jit(solution)/shard_map/psum | solution.py:56
  414.7 35.9 %all-gather = bf16[128,32,8]{1,2,0:T(8,128)(2,1)S(1)} all-gather(bf16[1,32,8]{1,2,0:T(8,128)(2,1)S(1)} %fusion.31), channel_id=1, replica_groups=mesh['leaf'=4,'rows'=32] {'leaf','rows'}, dimensions={0}, use_global_device_ids=true | all-gather | bytes 66048 | tf_op jit(solution)/shard_map/all_gather | solution.py:80
  450.9 3.2 fusion.13
  454.2 98.7 %all-reduce.11.cloned.1.call-done = f32[8,4096]{1,0:T(8,128)} async-done(((f32[8,4096]{1,0:T(8,128)}), f32[8,4096]{1,0:T(8,128)}) %all-reduce.11.cloned.1.call-update) | async-done | bytes 131088 | tf_op jit(solution)/shard_map/psum | solution.py:85
  553.8 1.3 copy.71
  555.1 2.0 gather_fusion
  557.1 1.0 fusion.14
  558.2 71.9 %reduce-scatter.9.cloned.1.call-done = f32[8,128]{1,0:T(8,128)} async-done(((f32[8,4096]{1,0:T(8,128)}), f32[8,128]{1,0:T(8,128)}) %reduce-scatter.9.cloned.1.call-update) | async-done | bytes 4112 | tf_op jit(solution)/shard_map/reduce_scatter | solution.py:91
  630.1 1.6 fusion.17
  631.7 73.8 %reduce-scatter.11.cloned.1.call-done = f32[8,128]{1,0:T(8,128)} async-done(((f32[8,4096]{1,0:T(8,128)}), f32[8,128]{1,0:T(8,128)}) %reduce-scatter.11.cloned.1.call-update) | async-done | bytes 4112 | tf_op jit(solution)/shard_map/reduce_scatter | solution.py:94
  706.2 23.5 %all_gather.23 = bf16[8,4096]{1,0:T(8,128)(2,1)S(1)} all-gather(bf16[8,128]{1,0:T(8,128)(2,1)S(1)} %convert_element_type.38), channel_id=1, replica_groups=mesh['leaf'=4,'rows'=32] {'rows'}, dimensions={1}, use_global_device_ids=true | all-gather | bytes 67584 | tf_op jit(solution)/shard_map/all_gather | solution.py:95
  730.7 3.2 gather_fusion.1
  734.1 2.8 convolution_bitcast_fusion.1
  736.9 3.1 copy.76
  740.0 4.5 reshape.143
  744.6 76.7 %reduce-scatter.13.cloned.1.call-done = f32[64,32]{1,0:T(8,128)} async-done(((f32[2048,32]{1,0:T(8,128)}), f32[64,32]{1,0:T(8,128)}) %reduce-scatter.13.cloned.1.call-update) | async-done | bytes 8208
  822.6 3.1 copy.78
  825.6 4.5 reshape.145
  830.2 1.3 constant_dynamic-slice_fusion
  831.6 76.0 %reduce-scatter.15.cloned.1.call-done = f32[64,32]{1,0:T(8,128)} async-done(((f32[2048,32]{1,0:T(8,128)}), f32[64,32]{1,0:T(8,128)}) %reduce-scatter.15.cloned.1.call-update) | async-done | bytes 8208
  (64 shorter events, 11.5 us)
Async XLA Ops:
  7.2 29.2 %copy-start = (bf16[4,64,2048]{2,1,0:T(8,128)(2,1)S(1)}, bf16[4,64,2048]{2,1,0:T(8,128)(2,1)}, u32[]{:S(2)}) copy-start(bf16[4,64,2048]{2,1,0:T(8,128)(2,1)} %param.15) | copy-start | bytes 3145732
  7.2 172.4 %all-reduce.5.cloned.1.call-start = ((), (), s32[]{:S(2)}) async-start(), calls=%async_computation.4 | async-start | bytes 524288 | tf_op jit(solution)/shard_map/psum | solution.py:54
  36.3 26.3 %copy-start.7 = (s32[4]{0:T(128)S(1)}, s32[4]{0:T(128)}, u32[]{:S(2)}) copy-start(s32[4]{0:T(128)} %param.18) | copy-start | bytes 52
  74.5 3.6 copy-start.8
  74.5 106.7 %copy-start.5 = (f32[8,1,128]{2,1,0:T(1,128)S(1)}, f32[8,1,128]{2,1,0:T(1,128)}, u32[]{:S(2)}) copy-start(f32[8,1,128]{2,1,0:T(1,128)} %param.13) | copy-start | bytes 12292
  74.5 131.4 %copy-start.3 = (bf16[1,128,4096]{2,1,0:T(8,128)(2,1)S(1)}, bf16[1,128,4096]{2,1,0:T(8,128)(2,1)}, u32[]{:S(2)}) copy-start(bf16[1,128,4096]{2,1,0:T(8,128)(2,1)} %param.19) | copy-start | bytes 3145732
  78.0 149.7 %copy-start.1 = (bf16[1,128,4096]{2,1,0:T(8,128)(2,1)S(1)}, bf16[1,128,4096]{2,1,0:T(8,128)(2,1)}, u32[]{:S(2)}) copy-start(bf16[1,128,4096]{2,1,0:T(8,128)(2,1)} %param.20) | copy-start | bytes 3145732
  78.1 294.8 %all-reduce.9.cloned.1.call-start = ((), (), s32[]{:S(2)}) async-start(), calls=%async_computation.6 | async-start | bytes 262144 | tf_op jit(solution)/shard_map/psum | solution.py:75
  228.2 185.7 %copy-start.6 = (f32[8,32]{1,0:T(8,128)S(1)}, f32[8,32]{1,0:T(8,128)}, u32[]{:S(2)}) copy-start(f32[8,32]{1,0:T(8,128)} %param.14) | copy-start | bytes 3076
  231.0 182.9 %all-reduce.7.cloned.1.call-start = ((), (), s32[]{:S(2)}) async-start(), calls=%async_computation.5 | async-start | bytes 262144 | tf_op jit(solution)/shard_map/psum | solution.py:56
  231.8 321.1 %all-reduce.11.cloned.1.call-start = ((), (), s32[]{:S(2)}) async-start(), calls=%async_computation.7 | async-start | bytes 262144 | tf_op jit(solution)/shard_map/psum | solution.py:85
  450.6 106.5 %copy-start.2 = (bf16[1,128,4096]{2,1,0:T(8,128)(2,1)S(1)}, bf16[1,128,4096]{2,1,0:T(8,128)(2,1)}, u32[]{:S(2)}) copy-start(bf16[1,128,4096]{2,1,0:T(8,128)(2,1)} %param.20) | copy-start | bytes 3145732
  450.9 179.2 %copy-start.4 = (bf16[1,128,4096]{2,1,0:T(8,128)(2,1)S(1)}, bf16[1,128,4096]{2,1,0:T(8,128)(2,1)}, u32[]{:S(2)}) copy-start(bf16[1,128,4096]{2,1,0:T(8,128)(2,1)} %param.19) | copy-start | bytes 3145732
  454.1 176.0 %reduce-scatter.9.cloned.1.call-start = ((), (), s32[]{:S(2)}) async-start(), calls=%async_computation.8 | async-start | bytes 135168 | tf_op jit(solution)/shard_map/reduce_scatter | solution.py:91
  558.1 147.3 %reduce-scatter.11.cloned.1.call-start = ((), (), s32[]{:S(2)}) async-start(), calls=%async_computation.9 | async-start | bytes 135168 | tf_op jit(solution)/shard_map/reduce_scatter | solution.py:94
  631.7 189.7 %reduce-scatter.13.cloned.1.call-start = ((), (), s32[]{:S(2)}) async-start(), calls=%async_computation.10 | async-start | bytes 1081344
  744.6 163.0 %reduce-scatter.15.cloned.1.call-start = ((), (), s32[]{:S(2)}) async-start(), calls=%async_computation.11 | async-start | bytes 1081344
Sparse Core Ops, SparseCore 0:
  78.2 101.3 all-reduce.4
  231.2 141.6 all-reduce.8
  375.1 38.7 all-reduce.6
  454.2 98.5 all-reduce.10
  558.3 71.7 reduce-scatter.8
  633.9 71.5 reduce-scatter.10
  744.7 76.6 reduce-scatter.12
  830.3 77.2 reduce-scatter.14
where the time goes:
time: 917 us; the launch traced here: 916 us
  waiting for transfers between devices  681 us (74%)
  blocking collectives  158 us (17%)
  local copies, waits for them, and re-layouts  35.6 us (4%)
  between operations  15 us (2%)
  matrix products  13.8 us (2%)
  other arithmetic  12.2 us (1%)
    unnamed x10, waiting for transfers between devices  154 us
    psum x1, waiting for transfers between devices, shards(): root_acc = root_from_leaves + lax.psum(parent_root, ('leaf', 'rows'))  141 us
    psum x1, waiting for transfers between devices, shards(): group_acc = lax.psum(local_acc, 'rows')  101 us
    psum x1, waiting for transfers between devices, shards(): root_full = lax.psum(root_term, 'rows')  98.7 us
    reduce_scatter x1, waiting for transfers between devices, shards(): lax.psum_scatter(parent_sol_term, 'rows', scatter_dimension=1, tiled=True)  73.8 us
    reduce_scatter x1, waiting for transfers between devices, shards(): lax.psum_scatter(parent_term, 'rows', scatter_dimension=1, tiled=True)  71.9 us
    psum x1, waiting for transfers between devices, shards(): root_from_leaves = lax.psum(group_acc[:, parent_width:], 'leaf')  41.1 us
    all_gather x1, blocking collectives, shards(): lax.all_gather(rrb, ('leaf', 'rows'), axis=1, tiled=True)  35.9 us
  transfers between devices with their start and end apart: 8, of which 8 were waited for; matrix products, arithmetic and copies ran while one was open for 0% of the time, Pallas kernels for 0%

commit v1 on v0

--- a/solution.py
+++ b/solution.py
@@ -2,6 +2,12 @@
 import jax.numpy as jnp
 from jax import lax
 from jax.sharding import PartitionSpec as P
+
+
+def obtain_face(z_in):
+    for k0 in ("leaf", "rows"):
+        z_in = jax.lax.psum(z_in, k0)
+    return z_in
 
 
 def shards(
@@ -72,7 +78,7 @@
     parent_mask = parent_pos < parent_height[0]
     pupd = jnp.where(parent_mask[None, :], pupd, 0.0)
     parent_root = jnp.zeros((rcount, root_width), jnp.float32).at[:, parent_rows[0]].add(pupd)
-    root_acc = root_from_leaves + lax.psum(parent_root, ("leaf", "rows"))
+    root_acc = root_from_leaves + obtain_face(parent_root)
     root_slice = lax.dynamic_slice_in_dim(root_acc, flat_index * root_cols, root_cols, 1)
     rrb = (root_rhs - root_slice).astype(jnp.bfloat16)
     block = root_inv

time: 917 us -> 880 us (0.960)
  waiting for transfers between devices: 681 us -> 644 us
    psum x2, waiting for transfers between devices: 182 us -> 146 us  [obtain_face(): z_in = jax.lax.psum(z_in, k0)]
where the time goes in v1:
time: 880 us
  waiting for transfers between devices  644 us (73%)
  blocking collectives  159 us (18%)
  local copies, waits for them, and re-layouts  35.5 us (4%)
  between operations  15 us (2%)
  matrix products  13.8 us (2%)
  other arithmetic  12.2 us (1%)
    unnamed x10, waiting for transfers between devices  153 us
    psum x2, waiting for transfers between devices, obtain_face(): z_in = jax.lax.psum(z_in, k0)  146 us
    psum x1, waiting for transfers between devices, shards(): group_acc = lax.psum(local_acc, 'rows')  101 us
    psum x1, waiting for transfers between devices, shards(): root_full = lax.psum(root_term, 'rows')  98.3 us
    reduce_scatter x1, waiting for transfers between devices, shards(): lax.psum_scatter(parent_sol_term, 'rows', scatter_dimension=1, tiled=True)  73.7 us
    reduce_scatter x1, waiting for transfers between devices, shards(): lax.psum_scatter(parent_term, 'rows', scatter_dimension=1, tiled=True)  71.9 us
    all_gather x1, blocking collectives, shards(): lax.all_gather(rrb, ('leaf', 'rows'), axis=1, tiled=True)  36.4 us
    all_gather x1, blocking collectives, shards(): lax.all_gather(leaf_rhs.astype(jnp.bfloat16), 'rows', axis=2, tiled=True)  27.5 us
  transfers between devices with their start and end apart: 8, of which 8 were waited for; matrix products, arithmetic and copies ran while one was open for 0% of the time, Pallas kernels for 0%

profile of v1, /device:TPU:0, one launch (start us, length us, event | category | flops | bytes accessed | tf_op | source)
XLA Modules:
  0.0 879.7 jit_solution(1502519760044363096)
XLA Ops:
  8.9 27.5 %all_gather.18 = bf16[8,4,2048]{0,1,2:T(4,128)(2,1)S(1)} all-gather(bf16[8,4,64]{0,1,2:T(4,128)(2,1)S(1)} %copy.62), channel_id=1, replica_groups=mesh['leaf'=4,'rows'=32] {'rows'}, dimensions={2}, use_global_device_ids=true | all-gather | bytes 135168 | tf_op jit(solution)/shard_map/all_gather | solution.py:39
  37.3 25.3 %all_gather.19 = bf16[8,4,2048]{0,1,2:T(4,128)(2,1)S(1)} all-gather(bf16[8,4,64]{0,1,2:T(4,128)(2,1)S(1)} %copy.64), channel_id=1, replica_groups=mesh['leaf'=4,'rows'=32] {'rows'}, dimensions={2}, use_global_device_ids=true | all-gather | bytes 135168 | tf_op jit(solution)/shard_map/all_gather | solution.py:47
  62.7 3.4 fusion.6
  66.3 8.2 scatter_custom_fusion
  74.5 3.5 copy.67
  78.9 100.7 %all-reduce.6.cloned.1.call-done = f32[8,8192]{1,0:T(8,128)} async-done(((f32[8,8192]{1,0:T(8,128)}), f32[8,8192]{1,0:T(8,128)}) %all-reduce.6.cloned.1.call-update) | async-done | bytes 262160 | tf_op jit(solution)/shard_map/psum | solution.py:60
  179.6 1.6 fusion.35
  181.2 24.6 %all_gather.20 = bf16[8,4096]{1,0:T(8,128)(2,1)S(1)} all-gather(bf16[8,128]{1,0:T(8,128)(2,1)S(1)} %subtract_convert_fusion.3), channel_id=1, replica_groups=mesh['leaf'=4,'rows'=32] {'rows'}, dimensions={1}, use_global_device_ids=true | all-gather | bytes 67584 | tf_op jit(solution)/shard_map/all_gather | solution.py:69
  206.2 21.5 %all_gather.21 = bf16[8,4096]{1,0:T(8,128)(2,1)S(1)} all-gather(bf16[8,128]{1,0:T(8,128)(2,1)S(1)} %get-tuple-element.24), channel_id=1, replica_groups=mesh['leaf'=4,'rows'=32] {'rows'}, dimensions={1}, use_global_device_ids=true | all-gather | bytes 67584 | tf_op jit(solution)/shard_map/all_gather | solution.py:75
  228.2 1.5 scatter_custom_fusion.1
  229.8 1.2 copy.69
  231.1 41.5 %all-reduce.12.cloned.1.call-done = (f32[8,4096]{1,0:T(8,128)}, f32[8,4096]{1,0:T(8,128)}) async-done(((f32[8,4096]{1,0:T(8,128)}, f32[8,4096]{1,0:T(8,128)}), (f32[8,4096]{1,0:T(8,128)}, f32[8,4096]{1,0:T(8,128)})) %all-reduce.12.cloned.1.call-update) | async-done | bytes 262160 | tf_op jit(solution)/shard_map/psum | solution.py:9
  272.6 104.8 %all-reduce.8.cloned.1.call-done = f32[8,4096]{1,0:T(8,128)} async-done(((f32[8,4096]{1,0:T(8,128)}), f32[8,4096]{1,0:T(8,128)}) %all-reduce.8.cloned.1.call-update) | async-done | bytes 131088 | tf_op jit(solution)/shard_map/psum | solution.py:9
  378.2 36.4 %all-gather = bf16[128,32,8]{1,2,0:T(8,128)(2,1)S(1)} all-gather(bf16[1,32,8]{1,2,0:T(8,128)(2,1)S(1)} %fusion.31), channel_id=1, replica_groups=mesh['leaf'=4,'rows'=32] {'leaf','rows'}, dimensions={0}, use_global_device_ids=true | all-gather | bytes 66048 | tf_op jit(solution)/shard_map/all_gather | solution.py:86
  415.0 3.2 fusion.13
  418.3 98.3 %all-reduce.10.cloned.1.call-done = f32[8,4096]{1,0:T(8,128)} async-done(((f32[8,4096]{1,0:T(8,128)}), f32[8,4096]{1,0:T(8,128)}) %all-reduce.10.cloned.1.call-update) | async-done | bytes 131088 | tf_op jit(solution)/shard_map/psum | solution.py:91
  517.5 1.3 copy.71
  518.8 2.0 gather_fusion
  520.8 1.0 fusion.14
  521.9 71.9 %reduce-scatter.9.cloned.1.call-done = f32[8,128]{1,0:T(8,128)} async-done(((f32[8,4096]{1,0:T(8,128)}), f32[8,128]{1,0:T(8,128)}) %reduce-scatter.9.cloned.1.call-update) | async-done | bytes 4112 | tf_op jit(solution)/shard_map/reduce_scatter | solution.py:97
  593.8 1.6 fusion.17
  595.5 73.7 %reduce-scatter.11.cloned.1.call-done = f32[8,128]{1,0:T(8,128)} async-done(((f32[8,4096]{1,0:T(8,128)}), f32[8,128]{1,0:T(8,128)}) %reduce-scatter.11.cloned.1.call-update) | async-done | bytes 4112 | tf_op jit(solution)/shard_map/reduce_scatter | solution.py:100
  669.9 23.5 %all_gather.23 = bf16[8,4096]{1,0:T(8,128)(2,1)S(1)} all-gather(bf16[8,128]{1,0:T(8,128)(2,1)S(1)} %convert_element_type.38), channel_id=1, replica_groups=mesh['leaf'=4,'rows'=32] {'rows'}, dimensions={1}, use_global_device_ids=true | all-gather | bytes 67584 | tf_op jit(solution)/shard_map/all_gather | solution.py:101
  694.5 3.2 gather_fusion.1
  697.8 2.8 convolution_bitcast_fusion.1
  700.6 3.1 copy.76
  703.7 4.5 reshape.143
  708.3 76.7 %reduce-scatter.13.cloned.1.call-done = f32[64,32]{1,0:T(8,128)} async-done(((f32[2048,32]{1,0:T(8,128)}), f32[64,32]{1,0:T(8,128)}) %reduce-scatter.13.cloned.1.call-update) | async-done | bytes 8208
  786.2 3.1 copy.78
  789.3 4.5 reshape.145
  793.9 1.4 constant_dynamic-slice_fusion
  795.2 76.0 %reduce-scatter.15.cloned.1.call-done = f32[64,32]{1,0:T(8,128)} async-done(((f32[2048,32]{1,0:T(8,128)}), f32[64,32]{1,0:T(8,128)}) %reduce-scatter.15.cloned.1.call-update) | async-done | bytes 8208
  (64 shorter events, 10.8 us)
Async XLA Ops:
  7.2 29.2 %copy-start = (bf16[4,64,2048]{2,1,0:T(8,128)(2,1)S(1)}, bf16[4,64,2048]{2,1,0:T(8,128)(2,1)}, u32[]{:S(2)}) copy-start(bf16[4,64,2048]{2,1,0:T(8,128)(2,1)} %param.15) | copy-start | bytes 3145732
  7.2 172.4 %all-reduce.6.cloned.1.call-start = ((), (), s32[]{:S(2)}) async-start(), calls=%async_computation.4 | async-start | bytes 524288 | tf_op jit(solution)/shard_map/psum | solution.py:60
  36.3 26.3 %copy-start.7 = (s32[4]{0:T(128)S(1)}, s32[4]{0:T(128)}, u32[]{:S(2)}) copy-start(s32[4]{0:T(128)} %param.18) | copy-start | bytes 52
  74.5 3.6 copy-start.8
  74.5 106.7 %copy-start.5 = (f32[8,1,128]{2,1,0:T(1,128)S(1)}, f32[8,1,128]{2,1,0:T(1,128)}, u32[]{:S(2)}) copy-start(f32[8,1,128]{2,1,0:T(1,128)} %param.13) | copy-start | bytes 12292
  74.5 131.4 %copy-start.3 = (bf16[1,128,4096]{2,1,0:T(8,128)(2,1)S(1)}, bf16[1,128,4096]{2,1,0:T(8,128)(2,1)}, u32[]{:S(2)}) copy-start(bf16[1,128,4096]{2,1,0:T(8,128)(2,1)} %param.19) | copy-start | bytes 3145732
  78.0 149.7 %copy-start.1 = (bf16[1,128,4096]{2,1,0:T(8,128)(2,1)S(1)}, bf16[1,128,4096]{2,1,0:T(8,128)(2,1)}, u32[]{:S(2)}) copy-start(bf16[1,128,4096]{2,1,0:T(8,128)(2,1)} %param.20) | copy-start | bytes 3145732
  78.1 194.5 %all-reduce.12.cloned.1.call-start = ((), (), s32[]{:S(2)}) async-start(), calls=%async_computation.11 | async-start | bytes 524288 | tf_op jit(solution)/shard_map/psum | solution.py:9
  228.2 149.3 %copy-start.6 = (f32[8,32]{1,0:T(8,128)S(1)}, f32[8,32]{1,0:T(8,128)}, u32[]{:S(2)}) copy-start(f32[8,32]{1,0:T(8,128)} %param.14) | copy-start | bytes 3076
  231.0 146.5 %all-reduce.8.cloned.1.call-start = ((), (), s32[]{:S(2)}) async-start(), calls=%async_computation.5 | async-start | bytes 262144 | tf_op jit(solution)/shard_map/psum | solution.py:9
  272.6 244.0 %all-reduce.10.cloned.1.call-start = ((), (), s32[]{:S(2)}) async-start(), calls=%async_computation.6 | async-start | bytes 262144 | tf_op jit(solution)/shard_map/psum | solution.py:91
  414.7 106.1 %copy-start.2 = (bf16[1,128,4096]{2,1,0:T(8,128)(2,1)S(1)}, bf16[1,128,4096]{2,1,0:T(8,128)(2,1)}, u32[]{:S(2)}) copy-start(bf16[1,128,4096]{2,1,0:T(8,128)(2,1)} %param.20) | copy-start | bytes 3145732
  415.0 178.8 %copy-start.4 = (bf16[1,128,4096]{2,1,0:T(8,128)(2,1)S(1)}, bf16[1,128,4096]{2,1,0:T(8,128)(2,1)}, u32[]{:S(2)}) copy-start(bf16[1,128,4096]{2,1,0:T(8,128)(2,1)} %param.19) | copy-start | bytes 3145732
  418.2 175.6 %reduce-scatter.9.cloned.1.call-start = ((), (), s32[]{:S(2)}) async-start(), calls=%async_computation.7 | async-start | bytes 135168 | tf_op jit(solution)/shard_map/reduce_scatter | solution.py:97
  521.9 147.3 %reduce-scatter.11.cloned.1.call-start = ((), (), s32[]{:S(2)}) async-start(), calls=%async_computation.8 | async-start | bytes 135168 | tf_op jit(solution)/shard_map/reduce_scatter | solution.py:100
  595.4 189.6 %reduce-scatter.13.cloned.1.call-start = ((), (), s32[]{:S(2)}) async-start(), calls=%async_computation.9 | async-start | bytes 1081344
  708.2 163.0 %reduce-scatter.15.cloned.1.call-start = ((), (), s32[]{:S(2)}) async-start(), calls=%async_computation.10 | async-start | bytes 1081344
Sparse Core Ops, SparseCore 0:
  78.2 101.3 all-reduce.5
  231.1 41.3 all-reduce.11
  275.8 101.6 all-reduce.7
  418.3 98.1 all-reduce.9
  522.0 71.7 reduce-scatter.8
  597.6 71.5 reduce-scatter.10
  708.4 76.6 reduce-scatter.12
  794.0 77.2 reduce-scatter.14
